TPU v7x, 32 devices: a whole 2x2x4 slice. The times are simulated.
32 devices in a mesh: pts: 8 (over y, x, core), val: 4 (over z).
Axes of the slice: x: 2, y: 2, z: 4, core: 2. Of those that a mesh axis runs over, the one named last changes fastest.
Arguments:
- vectors: float32 [1, 512, 2048], P(None, 'val', 'pts'), may hold values from -6 to 6
- eval_energy: float32 [512], P('val'), may hold values from -2 to -0.2
- cond_energy: float32 [2048], P('pts'), may hold values from 0.2 to 2
- val_orbitals: float32 [512, 8192], P('pts', 'val'), may hold values from -0.25 to 0.25
- cond_orbitals: float32 [2048, 8192], P('val', 'pts'), may hold values from -0.125 to 0.125
- screened: float32 [8192, 8192], P('val', 'pts'), may hold values from -1.5 to 1.5
Outputs:
- filtered: float32 [1, 512, 2048], P(None, 'val', 'pts')
All inputs are finite; a program needn't handle non-finite values.
Results may differ from a plain program's by a relative error of at most 0.00013.
Values sent between devices are 32-bit elements; how exact they have to be, the bound alone decides.
A program may use at most 128 MiB of HBM per device.

v0:
```python
import jax
import jax.numpy as jnp
from jax import lax
from jax.sharding import PartitionSpec as P

ITERS = 2
CENTER = 2.2
HALF_WIDTH = 2.0


def per_device(vectors, eval_energy, cond_energy, val_orbitals, cond_orbitals, screened):
    highest = lax.Precision.HIGHEST
    cond_whole = lax.all_gather(cond_orbitals, "val", axis=0, tiled=True)
    val_whole = lax.all_gather(val_orbitals, "pts", axis=0, tiled=True)
    ediff = cond_energy[None, None, :] - eval_energy[None, :, None]
    older = vectors
    newer = vectors
    for step in range(ITERS):
        direct_full_x = lax.all_gather(newer, "pts", axis=2, tiled=True)
        pair = jnp.einsum(
            "bvc,cn->bvn",
            direct_full_x,
            cond_whole,
            precision=highest,
            preferred_element_type=jnp.float32,
        )
        pair_all = lax.all_gather(pair, "val", axis=1, tiled=True)
        mixed = jnp.einsum(
            "vm,bvn->bmn",
            val_whole,
            pair_all,
            precision=highest,
            preferred_element_type=jnp.float32,
        )
        weighted = mixed * screened[None, :, :]
        back_terms = jnp.einsum(
            "vm,bmn->bvn",
            val_whole,
            weighted,
            precision=highest,
            preferred_element_type=jnp.float32,
        )
        back = lax.psum_scatter(back_terms, "val", scatter_dimension=1, tiled=True)
        hamil = ediff * newer - lax.psum_scatter(
            jnp.einsum(
                "bvn,cn->bvc",
                back,
                cond_whole,
                precision=highest,
                preferred_element_type=jnp.float32,
            ),
            "pts",
            scatter_dimension=2,
            tiled=True,
        )
        scaled = (hamil - CENTER * newer) / HALF_WIDTH
        if step == 0:
            following = scaled
        else:
            following = 2.0 * scaled - older
        older = newer
        newer = following
    return newer


def solution(mesh):
    placed = (
        P(None, "val", "pts"),
        P("val"),
        P("pts"),
        P("pts", "val"),
        P("val", "pts"),
        P("val", "pts"),
    )
    return jax.shard_map(
        per_device, mesh=mesh, in_specs=placed, out_specs=P(None, "val", "pts"), check_vma=False
    )
```

profile of v0, /device:TPU:0, one launch (start us, length us, event | category | flops | bytes accessed | tf_op | source)
XLA Modules:
  0.0 608.8 jit_solution(13954029730441035257)
XLA Ops:
  6.5 0.0 all-gather.9.cloned.1.call-start
  6.5 0.7 all-gather.9.cloned.1.call-update
  7.3 0.0 all-gather.11.cloned.1.call-start
  7.3 0.7 all-gather.11.cloned.1.call-update
  8.0 0.0 all-gather.13.cloned.1.call-start
  8.1 0.7 all-gather.13.cloned.1.call-update
  8.7 0.0 all-gather.17.cloned.1.call-start
  8.8 26.7 %all-gather.9.cloned.1.call-done = f32[1,128,2048]{2,1,0:T(8,128)} async-done(((f32[1,128,256]{2,1,0:T(8,128)}), f32[1,128,2048]{2,1,0:T(8,128)}) %all-gather.9.cloned.1.call-update) | async-done | bytes 1048592 | tf_op jit(solution)/shard_map/all_gather | solution.py:19
  35.4 151.2 %all-gather.11.cloned.1.call-done = f32[2048,1024]{1,0:T(8,128)} async-done(((f32[512,1024]{1,0:T(8,128)}), f32[2048,1024]{1,0:T(8,128)}) %all-gather.11.cloned.1.call-update) | async-done | bytes 8388624 | tf_op jit(solution)/shard_map/all_gather | solution.py:13
  186.7 9.2 %fusion.16 = f32[128,1024]{1,0:T(8,128)} fusion(f32[2048,1024]{1,0:T(8,128)} %all-gather.11.cloned.1.call-done, f32[1,128,2048]{2,1,0:T(8,128)} %all-gather.9.cloned.1.call-done), kind=kOutput, calls=%fused_computation.14 | convolution fusion | flops 3221225472 | bytes 9961472 | tf_op jit(solution)/shard_map/bvc,cn->bvn/dot_general | solution.py:20
  195.8 0.0 all-gather.17.cloned.1.call-update
  195.8 0.2 reduce-scatter.5.cloned.1.call-start
  196.1 9.1 %copy.7 = f32[2048,1024]{0,1:T(8,128)} copy(f32[2048,1024]{1,0:T(8,128)} %param.11) | data formatting | bytes 16777216 | tf_op args[5]
  205.2 18.1 %all-gather.13.cloned.1.call-done = f32[512,2048]{1,0:T(8,128)} async-done(((f32[64,2048]{1,0:T(8,128)}), f32[512,2048]{1,0:T(8,128)}) %all-gather.13.cloned.1.call-update) | async-done | bytes 4194320 | tf_op jit(solution)/shard_map/all_gather | solution.py:14
  223.3 47.1 %all-gather.17.cloned.1.call-done = f32[512,1024]{1,0:T(8,128)} async-done(((f32[128,1024]{1,0:T(8,128)}), f32[512,1024]{1,0:T(8,128)}) %all-gather.17.cloned.1.call-update) | async-done | bytes 2097168 | tf_op jit(solution)/shard_map/all_gather | solution.py:27
  270.5 17.0 %fusion.26 = f32[1024,2048]{1,0:T(8,128)S(1)} fusion(f32[512,1024]{1,0:T(8,128)} %all-gather.17.cloned.1.call-done, f32[512,2048]{1,0:T(8,128)} %all-gather.13.cloned.1.call-done), kind=kOutput, calls=%fused_computation.26 | convolution fusion | flops 12884901888 | bytes 14680064 | tf_op jit(solution)/shard_map/vm,bvn->bmn/dot_general | solution.py:28
  287.4 0.0 copy-done
  287.4 0.0 copy-done.1
  287.5 15.3 %fusion.8 = f32[1,512,1024]{1,2,0:T(8,128)} fusion(f32[512,2048]{1,0:T(8,128)S(1)} %copy-done.1, f32[1024,2048]{1,0:T(8,128)S(1)} %fusion.26, f32[2048,1024]{0,1:T(8,128)S(1)} %copy-done), kind=kOutput, calls=%fused_computation.10 | convolution fusion | flops 12886999040 | bytes 23068672 | tf_op jit(solution)/shard_map/vm,bmn->bvn/dot_general | solution.py:36
  302.8 0.0 reduce-scatter.5.cloned.1.call-update
  302.8 0.3 reduce-scatter.7.cloned.1.call-start
  303.1 42.3 %reduce-scatter.5.cloned.1.call-done = f32[1,128,1024]{1,2,0:T(8,128)} async-done(((f32[1,512,1024]{1,2,0:T(8,128)}), f32[1,128,1024]{1,2,0:T(8,128)}) %reduce-scatter.5.cloned.1.call-update) | async-done | bytes 524304 | tf_op jit(solution)/shard_map/reduce_scatter | solution.py:43
  345.4 13.4 %convolution_bitcast_fusion.1 = f32[1,128,2048]{2,1,0:T(8,128)} fusion(f32[2048,1024]{1,0:T(8,128)} %all-gather.11.cloned.1.call-done, f32[1,128,1024]{1,2,0:T(8,128)} %reduce-scatter.5.cloned.1.call-done), kind=kOutput, calls=%fused_computation.9 | convolution fusion | flops 3221225472 | bytes 9961472 | tf_op jit(solution)/shard_map/bvn,cn->bvc/dot_general | solution.py:45
  358.8 0.0 reduce-scatter.7.cloned.1.call-update
  358.8 0.0 all-gather.15.cloned.1.call-start
  358.8 35.3 %reduce-scatter.7.cloned.1.call-done = f32[1,128,256]{2,1,0:T(8,128)} async-done(((f32[1,128,2048]{2,1,0:T(8,128)}), f32[1,128,256]{2,1,0:T(8,128)}) %reduce-scatter.7.cloned.1.call-update) | async-done | bytes 131088 | tf_op jit(solution)/shard_map/reduce_scatter | solution.py:44
  394.1 0.0 copy-done.3
  394.1 0.0 copy-done.5
  394.1 0.0 copy-done.6
  394.1 1.7 fusion.25
  395.8 0.0 all-gather.15.cloned.1.call-update
  395.8 0.0 all-gather.19.cloned.1.call-start
  395.8 23.6 %all-gather.15.cloned.1.call-done = f32[1,128,2048]{2,1,0:T(8,128)} async-done(((f32[1,128,256]{2,1,0:T(8,128)}), f32[1,128,2048]{2,1,0:T(8,128)}) %all-gather.15.cloned.1.call-update) | async-done | bytes 1048592 | tf_op jit(solution)/shard_map/all_gather | solution.py:19
  419.5 9.2 %fusion.14 = f32[128,1024]{1,0:T(8,128)} fusion(f32[2048,1024]{1,0:T(8,128)} %all-gather.11.cloned.1.call-done, f32[1,128,2048]{2,1,0:T(8,128)} %all-gather.15.cloned.1.call-done), kind=kOutput, calls=%fused_computation.12 | convolution fusion | flops 3221225472 | bytes 9961472 | tf_op jit(solution)/shard_map/bvc,cn->bvn/dot_general | solution.py:20
  428.6 0.0 all-gather.19.cloned.1.call-update
  428.7 0.4 reduce-scatter.9.cloned.1.call-start
  429.1 45.4 %all-gather.19.cloned.1.call-done = f32[512,1024]{1,0:T(8,128)} async-done(((f32[128,1024]{1,0:T(8,128)}), f32[512,1024]{1,0:T(8,128)}) %all-gather.19.cloned.1.call-update) | async-done | bytes 2097168 | tf_op jit(solution)/shard_map/all_gather | solution.py:27
  474.5 16.9 %fusion.27 = f32[1024,2048]{1,0:T(8,128)S(1)} fusion(f32[512,1024]{1,0:T(8,128)} %all-gather.19.cloned.1.call-done, f32[512,2048]{1,0:T(8,128)} %all-gather.13.cloned.1.call-done), kind=kOutput, calls=%fused_computation.27 | convolution fusion | flops 12884901888 | bytes 14680064 | tf_op jit(solution)/shard_map/vm,bvn->bmn/dot_general | solution.py:28
  491.4 0.0 copy-done.2
  491.4 17.3 %fusion.11 = f32[1,512,1024]{1,2,0:T(8,128)} fusion(f32[512,2048]{1,0:T(8,128)S(1)} %copy-done.2, f32[1024,2048]{1,0:T(8,128)S(1)} %fusion.27, f32[2048,1024]{0,1:T(8,128)} %copy.7), kind=kOutput, calls=%fused_computation.11 | convolution fusion | flops 12886999040 | bytes 23068672 | tf_op jit(solution)/shard_map/vm,bmn->bvn/dot_general | solution.py:36
  508.7 0.0 reduce-scatter.9.cloned.1.call-update
  508.7 0.2 reduce-scatter.11.cloned.1.call-start
  508.9 42.4 %reduce-scatter.9.cloned.1.call-done = f32[1,128,1024]{1,2,0:T(8,128)} async-done(((f32[1,512,1024]{1,2,0:T(8,128)}), f32[1,128,1024]{1,2,0:T(8,128)}) %reduce-scatter.9.cloned.1.call-update) | async-done | bytes 524304 | tf_op jit(solution)/shard_map/reduce_scatter | solution.py:43
  551.3 13.4 %convolution_bitcast_fusion = f32[1,128,2048]{2,1,0:T(8,128)} fusion(f32[2048,1024]{1,0:T(8,128)} %all-gather.11.cloned.1.call-done, f32[1,128,1024]{1,2,0:T(8,128)} %reduce-scatter.9.cloned.1.call-done), kind=kOutput, calls=%fused_computation.8 | convolution fusion | flops 3221225472 | bytes 9961472 | tf_op jit(solution)/shard_map/bvn,cn->bvc/dot_general | solution.py:45
  564.8 0.0 reduce-scatter.11.cloned.1.call-update
  564.8 35.3 %reduce-scatter.11.cloned.1.call-done = f32[1,128,256]{2,1,0:T(8,128)} async-done(((f32[1,128,2048]{2,1,0:T(8,128)}), f32[1,128,256]{2,1,0:T(8,128)}) %reduce-scatter.11.cloned.1.call-update) | async-done | bytes 131088 | tf_op jit(solution)/shard_map/reduce_scatter | solution.py:44
  600.1 0.0 copy-done.4
  600.1 1.7 fusion.24
  (7 shorter events, 0.0 us)
Async XLA Ops:
  6.5 28.9 %all-gather.9.cloned.1.call-start = ((), (), s32[]{:S(2)}) async-start(), calls=%async_computation.4 | async-start | bytes 1179648 | tf_op jit(solution)/shard_map/all_gather | solution.py:19
  7.3 179.4 %all-gather.11.cloned.1.call-start = ((), (), s32[]{:S(2)}) async-start(), calls=%async_computation.5 | async-start | bytes 10485760 | tf_op jit(solution)/shard_map/all_gather | solution.py:13
  8.0 215.3 %all-gather.13.cloned.1.call-start = ((), (), s32[]{:S(2)}) async-start(), calls=%async_computation.6 | async-start | bytes 4718592 | tf_op jit(solution)/shard_map/all_gather | solution.py:14
  8.7 261.7 %all-gather.17.cloned.1.call-start = ((), (), s32[]{:S(2)}) async-start(), calls=%async_computation.12 | async-start | bytes 2621440 | tf_op jit(solution)/shard_map/all_gather | solution.py:27
  195.8 149.5 %reduce-scatter.5.cloned.1.call-start = ((), (), s32[]{:S(2)}) async-start(), calls=%async_computation.7 | async-start | bytes 2621440 | tf_op jit(solution)/shard_map/reduce_scatter | solution.py:43
  270.5 17.0 %copy-start = (f32[2048,1024]{0,1:T(8,128)S(1)}, f32[2048,1024]{0,1:T(8,128)}, u32[]{:S(2)}) copy-start(f32[2048,1024]{0,1:T(8,128)} %copy.7) | copy-start | bytes 25165828
  270.5 17.0 %copy-start.1 = (f32[512,2048]{1,0:T(8,128)S(1)}, f32[512,2048]{1,0:T(8,128)}, u32[]{:S(2)}) copy-start(f32[512,2048]{1,0:T(8,128)} %all-gather.13.cloned.1.call-done) | copy-start | bytes 12582916
  302.8 91.3 %copy-start.3 = (f32[1,128,256]{2,1,0:T(8,128)S(1)}, f32[1,128,256]{2,1,0:T(8,128)}, u32[]{:S(2)}) copy-start(f32[1,128,256]{2,1,0:T(8,128)} %param.6) | copy-start | bytes 393220
  302.8 91.3 %copy-start.5 = (f32[256]{0:T(256)S(1)}, f32[256]{0:T(256)}, u32[]{:S(2)}) copy-start(f32[256]{0:T(256)} %param.8) | copy-start | bytes 3076
  302.8 91.3 %copy-start.6 = (f32[128]{0:T(128)S(1)}, f32[128]{0:T(128)}, u32[]{:S(2)}) copy-start(f32[128]{0:T(128)} %param.7) | copy-start | bytes 1540
  302.8 91.3 %reduce-scatter.7.cloned.1.call-start = ((), (), s32[]{:S(2)}) async-start(), calls=%async_computation.8 | async-start | bytes 1179648 | tf_op jit(solution)/shard_map/reduce_scatter | solution.py:44
  358.8 60.7 %all-gather.15.cloned.1.call-start = ((), (), s32[]{:S(2)}) async-start(), calls=%async_computation.9 | async-start | bytes 1179648 | tf_op jit(solution)/shard_map/all_gather | solution.py:19
  395.8 78.7 %all-gather.19.cloned.1.call-start = ((), (), s32[]{:S(2)}) async-start(), calls=%async_computation.13 | async-start | bytes 2621440 | tf_op jit(solution)/shard_map/all_gather | solution.py:27
  428.7 122.7 %reduce-scatter.9.cloned.1.call-start = ((), (), s32[]{:S(2)}) async-start(), calls=%async_computation.10 | async-start | bytes 2621440 | tf_op jit(solution)/shard_map/reduce_scatter | solution.py:43
  474.5 17.0 %copy-start.2 = (f32[512,2048]{1,0:T(8,128)S(1)}, f32[512,2048]{1,0:T(8,128)}, u32[]{:S(2)}) copy-start(f32[512,2048]{1,0:T(8,128)} %all-gather.13.cloned.1.call-done) | copy-start | bytes 12582916
  508.7 91.4 %copy-start.4 = (f32[1,128,256]{2,1,0:T(8,128)S(1)}, f32[1,128,256]{2,1,0:T(8,128)}, u32[]{:S(2)}) copy-start(f32[1,128,256]{2,1,0:T(8,128)} %reduce-scatter.7.cloned.1.call-done) | copy-start | bytes 393220
  508.7 91.4 %reduce-scatter.11.cloned.1.call-start = ((), (), s32[]{:S(2)}) async-start(), calls=%async_computation.11 | async-start | bytes 1179648 | tf_op jit(solution)/shard_map/reduce_scatter | solution.py:44
Sparse Core Ops, SparseCore 0:
  9.2 26.1 all-gather.8
  37.0 149.5 all-gather.10
  188.5 34.7 all-gather.12
  224.8 45.6 all-gather.16
  302.9 42.4 reduce-scatter.4
  358.9 35.1 reduce-scatter.6
  396.0 23.4 all-gather.14
  428.8 45.6 all-gather.18
  508.8 42.4 reduce-scatter.8
  564.9 35.1 reduce-scatter.10
where the time goes:
time: 613 us; the launch traced here: 609 us
  waiting for transfers between devices  470 us (77%)
  matrix products  112 us (18%)
  between operations  13.8 us (2%)
  local copies, waits for them, and re-layouts  9.17 us (1%)
    all_gather x1, waiting for transfers between devices, per_device(): cond_whole = lax.all_gather(cond_orbitals, 'val', axis=0, tiled=True)  151 us
    all_gather x2, waiting for transfers between devices, per_device(): pair_all = lax.all_gather(pair, 'val', axis=1, tiled=True)  92.5 us
    reduce_scatter x2, waiting for transfers between devices, per_device(): back = lax.psum_scatter(back_terms, 'val', scatter_dimension=1, tiled=True)  84.7 us
    reduce_scatter x2, waiting for transfers between devices, per_device(): lax.psum_scatter(jnp.einsum('bvn,cn->bvc', back, cond_whole, precision=hi...  70.5 us
    all_gather x2, waiting for transfers between devices, per_device(): direct_full_x = lax.all_gather(newer, 'pts', axis=2, tiled=True)  50.3 us
    dot_general x2, matrix products, per_device(): jnp.einsum('vm,bvn->bmn', val_whole, pair_all, precision=highest, preferr...  33.9 us
    dot_general x2, matrix products, per_device(): jnp.einsum('vm,bmn->bvn', val_whole, weighted, precision=highest, preferr...  32.6 us
    dot_general x2, matrix products, per_device(): jnp.einsum('bvn,cn->bvc', back, cond_whole, precision=highest, preferred_...  26.8 us
  transfers between devices with their start and end apart: 10, of which 10 were waited for; matrix products, arithmetic and copies ran while one was open for 3% of the time, Pallas kernels for 0%

commit v1 on v0

--- a/solution.py
+++ b/solution.py
@@ -24,14 +24,40 @@
             precision=highest,
             preferred_element_type=jnp.float32,
         )
-        pair_all = lax.all_gather(pair, "val", axis=1, tiled=True)
+        size, position, span = (lax.axis_size("val"), lax.axis_index("val"), pair.shape[1])
+        forward = [(i, (i + 1) % size) for i in range(size)]
+        left = [(i, (i - 1) % size) for i in range(size)]
+        middle = size // 2
+        from_left = from_right = pair
         mixed = jnp.einsum(
             "vm,bvn->bmn",
-            val_whole,
-            pair_all,
+            lax.dynamic_slice_in_dim(val_whole, position * span, pair.shape[1], axis=0),
+            pair,
             precision=highest,
             preferred_element_type=jnp.float32,
         )
+        for k in range(1, middle + 1):
+            from_left = lax.ppermute(from_left, "val", forward)
+            if k < size - middle:
+                from_right = lax.ppermute(from_right, "val", left)
+                mixed = mixed + jnp.einsum(
+                    "vm,bvn->bmn",
+                    lax.dynamic_slice_in_dim(
+                        val_whole, (position + k) % size * span, from_right.shape[1], axis=0
+                    ),
+                    from_right,
+                    precision=highest,
+                    preferred_element_type=jnp.float32,
+                )
+            mixed = mixed + jnp.einsum(
+                "vm,bvn->bmn",
+                lax.dynamic_slice_in_dim(
+                    val_whole, (position - k) % size * span, from_left.shape[1], axis=0
+                ),
+                from_left,
+                precision=highest,
+                preferred_element_type=jnp.float32,
+            )
         weighted = mixed * screened[None, :, :]
         back_terms = jnp.einsum(
             "vm,bmn->bvn",

time: 613 us -> 586 us (0.956)
  waiting for transfers between devices: 470 us -> 382 us
  matrix products: 112 us -> 162 us
  starting transfers between devices: 1.33 us -> 9.61 us
    all_gather x2 -> x0, waiting for transfers between devices: 92.5 us -> none  [per_device(): pair_all = lax.all_gather(pair, 'val', axis=1, tiled=True)]
    dot_general x2 -> x8, matrix products: 33.9 us -> 73.7 us  [the longest x4 36.3 us: per_device(): jnp.einsum('vm,bvn->bmn', lax.dynamic_slice_in_dim(val_whole, (position -...]
    dot_general x2, matrix products: 32.6 us -> 46.1 us  [per_device(): jnp.einsum('vm,bmn->bvn', val_whole, weighted, precision=highest, preferr...]
    ppermute x0 -> x6, starting transfers between devices: none -> 9.33 us  [the longest x2 6.09 us: per_device(): from_right = lax.ppermute(from_right, 'val', left)]
    ppermute x0 -> x6, waiting for transfers between devices: none -> 7.29 us  [the longest x4 6.43 us: per_device(): from_left = lax.ppermute(from_left, 'val', forward)]
  transfers between devices with their start and end apart: 10 -> 14, of which waited for: 10 -> 11; matrix products, arithmetic and copies ran while one was open for 3% -> 12% of each run, Pallas kernels for 0% -> 0%
where the time goes in v1:
time: 586 us; the launch traced here: 580 us
  waiting for transfers between devices  382 us (65%)
  matrix products  162 us (28%)
  between operations  13.8 us (2%)
  starting transfers between devices  9.61 us (2%)
  local copies, waits for them, and re-layouts  9.38 us (2%)
    all_gather x1, waiting for transfers between devices, per_device(): cond_whole = lax.all_gather(cond_orbitals, 'val', axis=0, tiled=True)  151 us
    reduce_scatter x2, waiting for transfers between devices, per_device(): back = lax.psum_scatter(back_terms, 'val', scatter_dimension=1, tiled=True)  84.7 us
    reduce_scatter x2, waiting for transfers between devices, per_device(): lax.psum_scatter(jnp.einsum('bvn,cn->bvc', back, cond_whole, precision=hi...  70.6 us
    all_gather x2, waiting for transfers between devices, per_device(): direct_full_x = lax.all_gather(newer, 'pts', axis=2, tiled=True)  50.2 us
    dot_general x2, matrix products, per_device(): jnp.einsum('vm,bmn->bvn', val_whole, weighted, precision=highest, preferr...  46.1 us
    dot_general x4, matrix products, per_device(): jnp.einsum('vm,bvn->bmn', lax.dynamic_slice_in_dim(val_whole, (position -...  36.3 us
    dot_general x2, matrix products, per_device(): jnp.einsum('bvn,cn->bvc', back, cond_whole, precision=highest, preferred_...  26.8 us
    dot_general x2, matrix products, per_device(): jnp.einsum('vm,bvn->bmn', lax.dynamic_slice_in_dim(val_whole, position *...  19.3 us
  transfers between devices with their start and end apart: 14, of which 11 were waited for; matrix products, arithmetic and copies ran while one was open for 12% of the time, Pallas kernels for 0%

profile of v1, /device:TPU:0, one launch (start us, length us, event | category | flops | bytes accessed | tf_op | source)
XLA Modules:
  0.0 580.3 jit_solution(9048624216514535920)
XLA Ops:
  6.5 0.7 all-gather.5.cloned.1.call-update
  7.3 0.0 all-gather.7.cloned.1.call-start
  7.3 0.7 all-gather.7.cloned.1.call-update
  8.0 0.0 all-gather.9.cloned.1.call-start
  8.1 0.7 all-gather.9.cloned.1.call-update
  8.7 0.0 reduce-scatter.5.cloned.1.call-start
  8.8 26.7 %all-gather.5.cloned.1.call-done = f32[1,128,2048]{2,1,0:T(8,128)} async-done(((f32[1,128,256]{2,1,0:T(8,128)}), f32[1,128,2048]{2,1,0:T(8,128)}) %all-gather.5.cloned.1.call-update) | async-done | bytes 1048592 | tf_op jit(solution)/shard_map/all_gather | solution.py:19
  35.4 151.2 %all-gather.7.cloned.1.call-done = f32[2048,1024]{1,0:T(8,128)} async-done(((f32[512,1024]{1,0:T(8,128)}), f32[2048,1024]{1,0:T(8,128)}) %all-gather.7.cloned.1.call-update) | async-done | bytes 8388624 | tf_op jit(solution)/shard_map/all_gather | solution.py:13
  186.7 7.5 %fusion.22 = f32[128,1024]{1,0:T(8,128)S(1)} fusion(f32[2048,1024]{1,0:T(8,128)} %all-gather.7.cloned.1.call-done, f32[1,128,2048]{2,1,0:T(8,128)} %all-gather.5.cloned.1.call-done), kind=kOutput, calls=%fused_computation.20 | convolution fusion | flops 3221225472 | bytes 9961472 | tf_op jit(solution)/shard_map/bvc,cn->bvn/dot_general | solution.py:20
  194.2 0.1 collective-permute-start.1
  194.3 9.4 %copy.7 = f32[2048,1024]{0,1:T(8,128)} copy(f32[2048,1024]{1,0:T(8,128)} %param.11) | data formatting | bytes 16777216 | tf_op args[5]
  203.6 3.7 collective-permute-start
  207.4 16.0 %all-gather.9.cloned.1.call-done = f32[512,2048]{1,0:T(8,128)} async-done(((f32[64,2048]{1,0:T(8,128)}), f32[512,2048]{1,0:T(8,128)}) %all-gather.9.cloned.1.call-update) | async-done | bytes 4194320 | tf_op jit(solution)/shard_map/all_gather | solution.py:14
  223.3 10.2 %fusion.38 = f32[1024,2048]{1,0:T(8,128)} fusion(f32[128,1024]{1,0:T(8,128)S(1)} %fusion.22, f32[512,2048]{1,0:T(8,128)} %all-gather.9.cloned.1.call-done, s32[]{:T(128)S(6)} %select_n.37), kind=kOutput, calls=%fused_computation.36 | convolution fusion | flops 3221225472 | bytes 9961476 | tf_op jit(solution)/shard_map/vm,bvn->bmn/dot_general | solution.py:32
  233.6 1.6 collective-permute-start.2
  235.2 9.0 %fusion.30 = f32[1024,2048]{1,0:T(8,128)} fusion(f32[512,2048]{1,0:T(8,128)S(1)} %copy-done, s32[]{:T(128)S(6)} %select_n.41, f32[1,128,1024]{2,1,0:T(8,128)S(1)} %collective-permute-done.1), kind=kOutput, calls=%fused_computation.28 | convolution fusion | flops 3221225472 | bytes 9961476 | tf_op jit(solution)/shard_map/vm,bvn->bmn/dot_general | solution.py:52
  244.3 9.0 %fusion.34 = f32[1024,2048]{1,0:T(8,128)} fusion(f32[512,2048]{1,0:T(8,128)S(1)} %copy-done, s32[]{:T(128)S(6)} %select_n.39, f32[1,128,1024]{2,1,0:T(8,128)S(1)} %collective-permute-done), kind=kOutput, calls=%fused_computation.32 | convolution fusion | flops 3221225472 | bytes 9961476 | tf_op jit(solution)/shard_map/vm,bvn->bmn/dot_general | solution.py:43
  253.3 9.1 %fusion.26 = f32[1024,2048]{1,0:T(8,128)} fusion(f32[512,2048]{1,0:T(8,128)S(1)} %copy-done, s32[]{:T(128)S(6)} %select_n.43, f32[1,128,1024]{2,1,0:T(8,128)S(1)} %collective-permute-done.2), kind=kOutput, calls=%fused_computation.24 | convolution fusion | flops 3221225472 | bytes 9961476 | tf_op jit(solution)/shard_map/vm,bvn->bmn/dot_general | solution.py:52
  262.4 23.1 %fusion.14 = f32[1,512,1024]{1,2,0:T(8,128)} fusion(f32[512,2048]{1,0:T(8,128)} %all-gather.9.cloned.1.call-done, f32[2048,1024]{0,1:T(8,128)} %copy.7, f32[1024,2048]{1,0:T(8,128)} %fusion.26, f32[1024,2048]{1,0:T(8,128)} %fusion.30, f32[1024,2048]{1,0:T(8,128)} %fusion.38, f32[1024,2048]{1,0:T(8,128)} %fusion.34), kind=kOutput, calls=%fused_computation.16 | convolution fusion | flops 12893290496 | bytes 48234496 | tf_op jit(solution)/shard_map/vm,bmn->bvn/dot_general | solution.py:62
  285.6 0.0 reduce-scatter.5.cloned.1.call-update
  285.6 0.0 reduce-scatter.7.cloned.1.call-start
  285.6 42.8 %reduce-scatter.5.cloned.1.call-done = f32[1,128,1024]{1,2,0:T(8,128)} async-done(((f32[1,512,1024]{1,2,0:T(8,128)}), f32[1,128,1024]{1,2,0:T(8,128)}) %reduce-scatter.5.cloned.1.call-update) | async-done | bytes 524304 | tf_op jit(solution)/shard_map/reduce_scatter | solution.py:69
  328.4 13.4 %convolution_bitcast_fusion.1 = f32[1,128,2048]{2,1,0:T(8,128)} fusion(f32[2048,1024]{1,0:T(8,128)} %all-gather.7.cloned.1.call-done, f32[1,128,1024]{1,2,0:T(8,128)} %reduce-scatter.5.cloned.1.call-done), kind=kOutput, calls=%fused_computation.15 | convolution fusion | flops 3221225472 | bytes 9961472 | tf_op jit(solution)/shard_map/bvn,cn->bvc/dot_general | solution.py:71
  341.8 0.0 reduce-scatter.7.cloned.1.call-update
  341.8 0.0 all-gather.11.cloned.1.call-start
  341.9 35.3 %reduce-scatter.7.cloned.1.call-done = f32[1,128,256]{2,1,0:T(8,128)} async-done(((f32[1,128,2048]{2,1,0:T(8,128)}), f32[1,128,256]{2,1,0:T(8,128)}) %reduce-scatter.7.cloned.1.call-update) | async-done | bytes 131088 | tf_op jit(solution)/shard_map/reduce_scatter | solution.py:70
  377.2 1.7 fusion.53
  378.8 0.0 all-gather.11.cloned.1.call-update
  378.9 0.0 reduce-scatter.9.cloned.1.call-start
  378.9 23.6 %all-gather.11.cloned.1.call-done = f32[1,128,2048]{2,1,0:T(8,128)} async-done(((f32[1,128,256]{2,1,0:T(8,128)}), f32[1,128,2048]{2,1,0:T(8,128)}) %all-gather.11.cloned.1.call-update) | async-done | bytes 1048592 | tf_op jit(solution)/shard_map/all_gather | solution.py:19
  402.5 7.8 %fusion.20 = f32[128,1024]{1,0:T(8,128)S(1)} fusion(f32[2048,1024]{1,0:T(8,128)} %all-gather.7.cloned.1.call-done, f32[1,128,2048]{2,1,0:T(8,128)} %all-gather.11.cloned.1.call-done), kind=kOutput, calls=%fused_computation.18 | convolution fusion | flops 3221225472 | bytes 9961472 | tf_op jit(solution)/shard_map/bvc,cn->bvn/dot_general | solution.py:20
  410.3 1.5 collective-permute-start.4
  411.8 2.3 collective-permute-start.3
  414.2 9.1 %fusion.36 = f32[1024,2048]{1,0:T(8,128)} fusion(f32[128,1024]{1,0:T(8,128)S(1)} %fusion.20, f32[512,2048]{1,0:T(8,128)S(1)} %copy-done.1, s32[]{:T(128)S(6)} %select_n.37), kind=kOutput, calls=%fused_computation.34 | convolution fusion | flops 3221225472 | bytes 9961476 | tf_op jit(solution)/shard_map/vm,bvn->bmn/dot_general | solution.py:32
  423.3 3.7 collective-permute-done.4
  427.0 9.1 %fusion.28 = f32[1024,2048]{1,0:T(8,128)} fusion(f32[512,2048]{1,0:T(8,128)S(1)} %copy-done.1, s32[]{:T(128)S(6)} %select_n.41, f32[1,128,1024]{2,1,0:T(8,128)S(1)} %collective-permute-done.4), kind=kOutput, calls=%fused_computation.26 | convolution fusion | flops 3221225472 | bytes 9961476 | tf_op jit(solution)/shard_map/vm,bvn->bmn/dot_general | solution.py:52
  436.1 0.9 collective-permute-done.3
  436.9 9.1 %fusion.32 = f32[1024,2048]{1,0:T(8,128)} fusion(f32[512,2048]{1,0:T(8,128)S(1)} %copy-done.1, s32[]{:T(128)S(6)} %select_n.39, f32[1,128,1024]{2,1,0:T(8,128)S(1)} %collective-permute-done.3), kind=kOutput, calls=%fused_computation.30 | convolution fusion | flops 3221225472 | bytes 9961476 | tf_op jit(solution)/shard_map/vm,bvn->bmn/dot_general | solution.py:43
  446.0 2.7 collective-permute-done.5
  448.7 9.1 %fusion.24 = f32[1024,2048]{1,0:T(8,128)} fusion(f32[512,2048]{1,0:T(8,128)S(1)} %copy-done.1, s32[]{:T(128)S(6)} %select_n.43, f32[1,128,1024]{2,1,0:T(8,128)S(1)} %collective-permute-done.5), kind=kOutput, calls=%fused_computation.22 | convolution fusion | flops 3221225472 | bytes 9961476 | tf_op jit(solution)/shard_map/vm,bvn->bmn/dot_general | solution.py:52
  457.8 23.0 %fusion.17 = f32[1,512,1024]{1,2,0:T(8,128)} fusion(f32[512,2048]{1,0:T(8,128)} %all-gather.9.cloned.1.call-done, f32[2048,1024]{0,1:T(8,128)} %copy.7, f32[1024,2048]{1,0:T(8,128)} %fusion.24, f32[1024,2048]{1,0:T(8,128)} %fusion.28, f32[1024,2048]{1,0:T(8,128)} %fusion.36, f32[1024,2048]{1,0:T(8,128)} %fusion.32), kind=kOutput, calls=%fused_computation.17 | convolution fusion | flops 12893290496 | bytes 48234496 | tf_op jit(solution)/shard_map/vm,bmn->bvn/dot_general | solution.py:62
  480.8 0.0 reduce-scatter.9.cloned.1.call-update
  480.8 0.0 reduce-scatter.11.cloned.1.call-start
  480.9 41.9 %reduce-scatter.9.cloned.1.call-done = f32[1,128,1024]{1,2,0:T(8,128)} async-done(((f32[1,512,1024]{1,2,0:T(8,128)}), f32[1,128,1024]{1,2,0:T(8,128)}) %reduce-scatter.9.cloned.1.call-update) | async-done | bytes 524304 | tf_op jit(solution)/shard_map/reduce_scatter | solution.py:69
  522.7 13.4 %convolution_bitcast_fusion = f32[1,128,2048]{2,1,0:T(8,128)} fusion(f32[2048,1024]{1,0:T(8,128)} %all-gather.7.cloned.1.call-done, f32[1,128,1024]{1,2,0:T(8,128)} %reduce-scatter.9.cloned.1.call-done), kind=kOutput, calls=%fused_computation.14 | convolution fusion | flops 3221225472 | bytes 9961472 | tf_op jit(solution)/shard_map/bvn,cn->bvc/dot_general | solution.py:71
  536.1 0.0 reduce-scatter.11.cloned.1.call-update
  536.2 35.3 %reduce-scatter.11.cloned.1.call-done = f32[1,128,256]{2,1,0:T(8,128)} async-done(((f32[1,128,2048]{2,1,0:T(8,128)}), f32[1,128,256]{2,1,0:T(8,128)}) %reduce-scatter.11.cloned.1.call-update) | async-done | bytes 131088 | tf_op jit(solution)/shard_map/reduce_scatter | solution.py:70
  571.5 1.7 fusion.52
  (17 shorter events, 0.0 us)
Async XLA Ops:
  6.5 28.9 %all-gather.5.cloned.1.call-start = ((), (), s32[]{:S(2)}) async-start(), calls=%async_computation.4 | async-start | bytes 1179648 | tf_op jit(solution)/shard_map/all_gather | solution.py:19
  7.3 179.4 %all-gather.7.cloned.1.call-start = ((), (), s32[]{:S(2)}) async-start(), calls=%async_computation.5 | async-start | bytes 10485760 | tf_op jit(solution)/shard_map/all_gather | solution.py:13
  8.0 215.3 %all-gather.9.cloned.1.call-start = ((), (), s32[]{:S(2)}) async-start(), calls=%async_computation.6 | async-start | bytes 4718592 | tf_op jit(solution)/shard_map/all_gather | solution.py:14
  8.7 319.7 %reduce-scatter.5.cloned.1.call-start = ((), (), s32[]{:S(2)}) async-start(), calls=%async_computation.7 | async-start | bytes 2621440 | tf_op jit(solution)/shard_map/reduce_scatter | solution.py:69
  194.2 39.4 %collective-permute-start.1 = (f32[1,128,1024]{2,1,0:T(8,128)S(1)}, f32[1,128,1024]{2,1,0:T(8,128)S(1)}, u32[]{:S(2)}, u32[]{:S(2)}) collective-permute-start(f32[1,128,1024]{2,1,0:T(8,128)S(1)} %bitcast.93), channel_id=1, source_target_pairs={{0,1},{1,2},{2,3},{3,0},{4,5},{5,6},{6,7},{7,4},{8,9},{9,10},{10,1... | collective-permute-start | bytes 1572872 | tf_op jit(solution)/shard_map/ppermute | solution.py:40
  203.6 40.6 %collective-permute-start = (f32[1,128,1024]{2,1,0:T(8,128)S(1)}, f32[1,128,1024]{2,1,0:T(8,128)S(1)}, u32[]{:S(2)}, u32[]{:S(2)}) collective-permute-start(f32[1,128,1024]{2,1,0:T(8,128)S(1)} %bitcast.94), channel_id=1, source_target_pairs={{0,3},{1,0},{2,1},{3,2},{4,7},{5,4},{6,5},{7,6},{8,11},{9,8},{10,9... | collective-permute-start | bytes 1572872 | tf_op jit(solution)/shard_map/ppermute | solution.py:42
  223.3 11.9 %copy-start = (f32[512,2048]{1,0:T(8,128)S(1)}, f32[512,2048]{1,0:T(8,128)}, u32[]{:S(2)}) copy-start(f32[512,2048]{1,0:T(8,128)} %all-gather.9.cloned.1.call-done) | copy-start | bytes 12582916
  233.6 19.7 %collective-permute-start.2 = (f32[1,128,1024]{2,1,0:T(8,128)S(1)}, f32[1,128,1024]{2,1,0:T(8,128)S(1)}, u32[]{:S(2)}, u32[]{:S(2)}) collective-permute-start(f32[1,128,1024]{2,1,0:T(8,128)S(1)} %collective-permute-done.1), channel_id=1, source_target_pairs={{0,1},{1,2},{2,3},{3,0},{4,5},{5,6},{6,7},{7,4},{8,9},{9,10},{10,1... | collective-permute-start | bytes 1572872 | tf_op jit(solution)/shard_map/ppermute | solution.py:40
  285.5 91.6 %copy-start.2 = (f32[1,128,256]{2,1,0:T(8,128)S(1)}, f32[1,128,256]{2,1,0:T(8,128)}, u32[]{:S(2)}) copy-start(f32[1,128,256]{2,1,0:T(8,128)} %param.6) | copy-start | bytes 393220
  285.5 91.6 %copy-start.4 = (f32[256]{0:T(256)S(1)}, f32[256]{0:T(256)}, u32[]{:S(2)}) copy-start(f32[256]{0:T(256)} %param.8) | copy-start | bytes 3076
  285.5 91.6 %copy-start.5 = (f32[128]{0:T(128)S(1)}, f32[128]{0:T(128)}, u32[]{:S(2)}) copy-start(f32[128]{0:T(128)} %param.7) | copy-start | bytes 1540
  285.6 91.6 %reduce-scatter.7.cloned.1.call-start = ((), (), s32[]{:S(2)}) async-start(), calls=%async_computation.8 | async-start | bytes 1179648 | tf_op jit(solution)/shard_map/reduce_scatter | solution.py:70
  341.8 60.7 %all-gather.11.cloned.1.call-start = ((), (), s32[]{:S(2)}) async-start(), calls=%async_computation.9 | async-start | bytes 1179648 | tf_op jit(solution)/shard_map/all_gather | solution.py:19
  378.9 143.9 %reduce-scatter.9.cloned.1.call-start = ((), (), s32[]{:S(2)}) async-start(), calls=%async_computation.10 | async-start | bytes 2621440 | tf_op jit(solution)/shard_map/reduce_scatter | solution.py:69
  402.5 11.7 %copy-start.1 = (f32[512,2048]{1,0:T(8,128)S(1)}, f32[512,2048]{1,0:T(8,128)}, u32[]{:S(2)}) copy-start(f32[512,2048]{1,0:T(8,128)} %all-gather.9.cloned.1.call-done) | copy-start | bytes 12582916
  410.3 16.7 %collective-permute-start.4 = (f32[1,128,1024]{2,1,0:T(8,128)S(1)}, f32[1,128,1024]{2,1,0:T(8,128)S(1)}, u32[]{:S(2)}, u32[]{:S(2)}) collective-permute-start(f32[1,128,1024]{2,1,0:T(8,128)S(1)} %bitcast.95), channel_id=1, source_target_pairs={{0,1},{1,2},{2,3},{3,0},{4,5},{5,6},{6,7},{7,4},{8,9},{9,10},{10,1... | collective-permute-start | bytes 1572872 | tf_op jit(solution)/shard_map/ppermute | solution.py:40
  411.8 25.1 %collective-permute-start.3 = (f32[1,128,1024]{2,1,0:T(8,128)S(1)}, f32[1,128,1024]{2,1,0:T(8,128)S(1)}, u32[]{:S(2)}, u32[]{:S(2)}) collective-permute-start(f32[1,128,1024]{2,1,0:T(8,128)S(1)} %bitcast.96), channel_id=1, source_target_pairs={{0,3},{1,0},{2,1},{3,2},{4,7},{5,4},{6,5},{7,6},{8,11},{9,8},{10,9... | collective-permute-start | bytes 1572872 | tf_op jit(solution)/shard_map/ppermute | solution.py:42
  427.0 21.7 %collective-permute-start.5 = (f32[1,128,1024]{2,1,0:T(8,128)S(1)}, f32[1,128,1024]{2,1,0:T(8,128)S(1)}, u32[]{:S(2)}, u32[]{:S(2)}) collective-permute-start(f32[1,128,1024]{2,1,0:T(8,128)S(1)} %collective-permute-done.4), channel_id=1, source_target_pairs={{0,1},{1,2},{2,3},{3,0},{4,5},{5,6},{6,7},{7,4},{8,9},{9,10},{10,1... | collective-permute-start | bytes 1572872 | tf_op jit(solution)/shard_map/ppermute | solution.py:40
  480.8 90.7 %copy-start.3 = (f32[1,128,256]{2,1,0:T(8,128)S(1)}, f32[1,128,256]{2,1,0:T(8,128)}, u32[]{:S(2)}) copy-start(f32[1,128,256]{2,1,0:T(8,128)} %reduce-scatter.7.cloned.1.call-done) | copy-start | bytes 393220
  480.8 90.7 %reduce-scatter.11.cloned.1.call-start = ((), (), s32[]{:S(2)}) async-start(), calls=%async_computation.11 | async-start | bytes 1179648 | tf_op jit(solution)/shard_map/reduce_scatter | solution.py:70
Sparse Core Ops, SparseCore 0:
  9.2 26.1 all-gather.4
  37.0 149.5 all-gather.6
  188.5 34.7 all-gather.8
  285.7 42.6 reduce-scatter.4
  341.9 35.1 reduce-scatter.6
  379.0 23.4 all-gather.10
  480.9 41.7 reduce-scatter.8
  536.3 35.1 reduce-scatter.10
